TPU v7x, 128 devices: a whole 4x4x4 slice. The times are simulated.
128 devices in a mesh: leaf: 16 (over x, y), side: 8 (over z, core).
Axes of the slice: x: 4, y: 4, z: 4, core: 2. Of those that a mesh axis runs over, the one named last changes fastest.
Arguments:
- block: float32 [131072, 512], P(('leaf', 'side')), may hold values from -24 to 24
- basis: float32 [131072, 1024], P(('leaf', 'side')), may hold values from -1 to 1
Outputs:
- ortho: float32 [131072, 512], P(('leaf', 'side'))
- factor: float32 [512, 512], replicated
- coeffs: float32 [1024, 512], replicated
All inputs are finite; a program needn't handle non-finite values.
Results may differ from a plain program's by a relative error of at most 0.0001.
Values sent between devices are 32-bit elements; how exact they have to be, the bound alone decides.
A program may use at most 64 MiB of HBM per device.

v0:
```python
import jax
import jax.numpy as jnp
from jax import lax
from jax.sharding import PartitionSpec as P


def inner(left, right):
    return lax.dot_general(
        left,
        right,
        (((0,), (0,)), ((), ())),
        precision=lax.Precision.HIGHEST,
        preferred_element_type=jnp.float32,
    )


def product(left, right):
    return jnp.dot(left, right, precision=lax.Precision.HIGHEST, preferred_element_type=jnp.float32)


def small_upper(matrix):
    width = matrix.shape[0]
    positions = jnp.arange(width, dtype=jnp.int32)

    def one_step(column, carry):
        rest, result = carry
        column = jnp.asarray(column).astype(jnp.int32)
        row = lax.dynamic_slice_in_dim(rest, column, 1, 0)[0]
        pivot = jnp.sqrt(jnp.sum(jnp.where(positions == column, row, jnp.float32(0.0))))
        new_row = jnp.where(positions >= column, row / pivot, jnp.float32(0.0))
        result = lax.dynamic_update_slice_in_dim(result, new_row[None, :], column, 0)
        rest = rest - new_row[:, None] * new_row[None, :]
        return (rest, result)

    start = (matrix, jnp.zeros_like(matrix))
    return lax.fori_loop(0, width, one_step, start)[1]


def small_inverse(upper_block):
    width = upper_block.shape[0]
    positions = jnp.arange(width, dtype=jnp.int32)

    def one_step(count, result):
        index = (width - 1 - jnp.asarray(count)).astype(jnp.int32)
        row = lax.dynamic_slice_in_dim(upper_block, index, 1, 0)[0]
        pivot = jnp.sum(jnp.where(positions == index, row, jnp.float32(0.0)))
        beyond = jnp.where(positions > index, row, jnp.float32(0.0))
        unit = jnp.where(positions == index, jnp.float32(1.0), jnp.float32(0.0))
        new_row = (unit - product(beyond[None, :], result)[0]) / pivot
        return lax.dynamic_update_slice_in_dim(result, new_row[None, :], index, 0)

    return lax.fori_loop(0, width, one_step, jnp.zeros_like(upper_block))


def factor_and_inverse(gram):
    width = gram.shape[0]
    piece = min(128, width)
    count = width // piece
    rest = gram
    strips = []
    diag_inverses = []
    for index in range(count):
        diag = small_upper(rest[:piece, :piece])
        diag_inv = small_inverse(diag)
        right = product(diag_inv.T, rest[:piece, piece:])
        left_zeros = jnp.zeros((piece, index * piece), gram.dtype)
        strips.append(jnp.concatenate([left_zeros, diag, right], axis=1))
        diag_inverses.append(diag_inv)
        rest = rest[piece:, piece:] - inner(right, right)
    factor = jnp.concatenate(strips, axis=0)
    lower_part = None
    for index in reversed(range(count)):
        diag_inv = diag_inverses[index]
        if lower_part is None:
            lower_part = diag_inv
        else:
            coupling = factor[index * piece : (index + 1) * piece, (index + 1) * piece :]
            far = -product(diag_inv, product(coupling, lower_part))
            top = jnp.concatenate([diag_inv, far], axis=1)
            below = jnp.concatenate(
                [jnp.zeros((lower_part.shape[0], piece), gram.dtype), lower_part], axis=1
            )
            lower_part = jnp.concatenate([top, below], axis=0)
    return (factor, lower_part)


def shards(block, basis):
    rows_total = block.shape[0] * lax.axis_size("leaf") * lax.axis_size("side")
    coeffs = lax.psum(inner(basis, block), ("leaf", "side"))
    projected = block - product(basis, coeffs)
    local_gram = inner(projected, projected) / rows_total
    factor, inverse = factor_and_inverse(lax.psum(local_gram, ("leaf", "side")))
    ortho = product(projected, inverse)
    return (ortho, factor, coeffs)


def solution(mesh):
    return jax.shard_map(
        shards,
        mesh=mesh,
        in_specs=(P(("leaf", "side"), None), P(("leaf", "side"), None)),
        out_specs=(P(("leaf", "side"), None), P(), P()),
        check_vma=False,
    )
```

profile of v0, /device:TPU:1, one launch (start us, length us, event | category | flops | bytes accessed | tf_op | source)
XLA Modules:
  0.0 1886.3 jit_solution(14410040137876746820)
XLA Ops:
  7.2 10.2 fusion.74
  17.7 1.3 copy-done
  19.0 1.8 copy.5
  20.8 150.3 %all-reduce.7.cloned.1.call-done = f32[1024,512]{1,0:T(8,128)} async-done(((f32[1024,512]{1,0:T(8,128)}), f32[1024,512]{1,0:T(8,128)}) %all-reduce.7.cloned.1.call-update) | async-done | bytes 2097168 | tf_op jit(solution)/shard_map/psum | solution.py:89
  171.2 16.2 bitcast_subtract_fusion
  187.3 4.5 convolution_multiply_fusion
  191.8 145.8 %all-reduce.9.cloned.1.call-done = f32[512,512]{1,0:T(8,128)} async-done(((f32[512,512]{1,0:T(8,128)}), f32[512,512]{1,0:T(8,128)}) %all-reduce.9.cloned.1.call-update) | async-done | bytes 1048592 | tf_op jit(solution)/shard_map/psum | solution.py:92
  337.6 0.8 slice.36
  338.5 192.5 %while.136 = (s32[]{:T(128)}, f32[128,128]{1,0:T(8,128)S(1)}, f32[128,128]{1,0:T(8,128)S(1)}, s32[]{:T(128)}, s32[]{:T(128)}) while((s32[]{:T(128)}, f32[128,128]{1,0:T(8,128)S(1)}, f32[128,128]{1,0:T(8,128)S(1)}, s32[]{:T(128)}, s32[]{:T(128)}) %tuple.273), condition=%wide.region_4.5_spmd.clone.clone, body=%wide.region_2.4_spmd.clone.clone.sunk | while | flops 34305 | bytes 142421 | solution.py:36
  531.0 187.3 %while.137 = (s32[]{:T(128)}, f32[128,128]{1,0:T(8,128)S(1)}, f32[128,128]{1,0:T(8,128)S(1)}, s32[]{:T(128)}, s32[]{:T(128)}, /*index=5*/s32[]{:T(128)}, s32[]{:T(128)}) while((s32[]{:T(128)}, f32[128,128]{1,0:T(8,128)S(1)}, f32[128,128]{1,0:T(8,128)S(1)}, s32[]{:T(128)}, s32[]{:T(128)}, /*index=5*/s32[]{:T(128)}, ...), condition=%wide.region_7.8_spmd.clone.clone, body=%wide.region_5.7_spmd.clone.clone.sunk | while | flops 197765 | bytes 69783 | solution.py:52
  531.6 0.8 fusion.139
  557.9 0.8 fusion.139
  559.4 0.8 fusion.139
  585.7 0.8 fusion.139
  587.1 0.8 fusion.139
  613.4 0.8 fusion.139
  614.9 0.8 fusion.139
  641.2 0.8 fusion.139
  642.7 0.8 fusion.139
  669.0 0.8 fusion.139
  670.4 0.8 fusion.139
  696.8 0.8 fusion.139
  698.2 0.8 fusion.139
  718.9 1.3 fusion.63
  720.2 1.7 convolution_subtract_fusion
  722.0 192.5 %while.138 = (s32[]{:T(128)}, f32[128,128]{1,0:T(8,128)S(1)}, f32[128,128]{1,0:T(8,128)S(1)}, s32[]{:T(128)}, s32[]{:T(128)}) while((s32[]{:T(128)}, f32[128,128]{1,0:T(8,128)S(1)}, f32[128,128]{1,0:T(8,128)S(1)}, s32[]{:T(128)}, s32[]{:T(128)}) %tuple.279), condition=%wide.region_10.11_spmd.clone.clone, body=%wide.region_8.10_spmd.clone.clone.sunk | while | flops 34305 | bytes 142421 | solution.py:36
  914.5 187.1 %while.139 = (s32[]{:T(128)}, f32[128,128]{1,0:T(8,128)S(1)}, f32[128,128]{1,0:T(8,128)S(1)}, s32[]{:T(128)}, s32[]{:T(128)}, /*index=5*/s32[]{:T(128)}, s32[]{:T(128)}) while((s32[]{:T(128)}, f32[128,128]{1,0:T(8,128)S(1)}, f32[128,128]{1,0:T(8,128)S(1)}, s32[]{:T(128)}, s32[]{:T(128)}, /*index=5*/s32[]{:T(128)}, ...), condition=%wide.region_13.14_spmd.clone.clone, body=%wide.region_11.13_spmd.clone.clone.sunk | while | flops 197765 | bytes 69783 | solution.py:52
  918.0 0.8 fusion.145
  919.5 0.8 fusion.145
  945.8 0.8 fusion.145
  947.2 0.8 fusion.145
  973.5 0.8 fusion.145
  975.0 0.8 fusion.145
  1001.3 0.8 fusion.145
  1002.8 0.8 fusion.145
  1029.1 0.8 fusion.145
  1030.5 0.8 fusion.145
  1056.9 0.8 fusion.145
  1058.3 0.8 fusion.145
  1084.6 0.8 fusion.145
  1086.1 0.8 fusion.145
  1102.9 192.5 %while.140 = (s32[]{:T(128)}, f32[128,128]{1,0:T(8,128)S(1)}, f32[128,128]{1,0:T(8,128)S(1)}, s32[]{:T(128)}, s32[]{:T(128)}) while((s32[]{:T(128)}, f32[128,128]{1,0:T(8,128)S(1)}, f32[128,128]{1,0:T(8,128)S(1)}, s32[]{:T(128)}, s32[]{:T(128)}) %tuple.285), condition=%wide.region_16.17_spmd.clone.clone, body=%wide.region_14.16_spmd.clone.clone.sunk | while | flops 34305 | bytes 142421 | solution.py:36
  1295.4 187.1 %while.141 = (s32[]{:T(128)}, f32[128,128]{1,0:T(8,128)S(1)}, f32[128,128]{1,0:T(8,128)S(1)}, s32[]{:T(128)}, s32[]{:T(128)}, /*index=5*/s32[]{:T(128)}, s32[]{:T(128)}) while((s32[]{:T(128)}, f32[128,128]{1,0:T(8,128)S(1)}, f32[128,128]{1,0:T(8,128)S(1)}, s32[]{:T(128)}, s32[]{:T(128)}, /*index=5*/s32[]{:T(128)}, ...), condition=%wide.region_19.20_spmd.clone.clone, body=%wide.region_17.19_spmd.clone.clone.sunk | while | flops 197765 | bytes 69783 | solution.py:52
  1304.8 0.8 fusion.151
  1306.3 0.8 fusion.151
  1332.6 0.8 fusion.151
  1334.0 0.8 fusion.151
  1360.4 0.8 fusion.151
  1361.8 0.8 fusion.151
  1388.1 0.8 fusion.151
  1389.6 0.8 fusion.151
  1415.9 0.8 fusion.151
  1417.4 0.8 fusion.151
  1443.7 0.8 fusion.151
  1445.1 0.8 fusion.151
  1471.4 0.8 fusion.151
  1483.7 192.5 %while.142 = (s32[]{:T(128)}, f32[128,128]{1,0:T(8,128)S(1)}, f32[128,128]{1,0:T(8,128)S(1)}, s32[]{:T(128)}, s32[]{:T(128)}) while((s32[]{:T(128)}, f32[128,128]{1,0:T(8,128)S(1)}, f32[128,128]{1,0:T(8,128)S(1)}, s32[]{:T(128)}, s32[]{:T(128)}) %tuple.291), condition=%wide.region_22.23_spmd.clone.clone, body=%wide.region_20.22_spmd.clone.clone.sunk | while | flops 34305 | bytes 142421 | solution.py:36
  1676.3 187.1 %while.143 = (s32[]{:T(128)}, f32[128,128]{1,0:T(8,128)S(1)}, f32[128,128]{1,0:T(8,128)S(1)}, s32[]{:T(128)}, s32[]{:T(128)}, /*index=5*/s32[]{:T(128)}, s32[]{:T(128)}) while((s32[]{:T(128)}, f32[128,128]{1,0:T(8,128)S(1)}, f32[128,128]{1,0:T(8,128)S(1)}, s32[]{:T(128)}, s32[]{:T(128)}, /*index=5*/s32[]{:T(128)}, ...), condition=%wide.region_25.26_spmd.clone.clone, body=%wide.region_23.25_spmd.clone.clone.sunk | while | flops 197765 | bytes 69783 | solution.py:52
  1865.1 1.4 fusion.73
  1866.7 1.4 convolution_negate_fusion
  1868.2 8.0 fusion.56
  1876.2 1.1 select_maximum_fusion
  1877.3 0.8 copy-done.1
  1878.1 1.3 copy.83
  (4617 shorter events, 1100.8 us)
Async XLA Ops:
  7.2 164.0 %all-reduce.7.cloned.1.call-start = ((), (), s32[]{:S(2)}) async-start(), calls=%async_computation | async-start | bytes 4194304 | tf_op jit(solution)/shard_map/psum | solution.py:89
  17.4 1.6 copy-start
  17.4 320.2 %all-reduce.9.cloned.1.call-start = ((), (), s32[]{:S(2)}) async-start(), calls=%async_computation.1 | async-start | bytes 2097152 | tf_op jit(solution)/shard_map/psum | solution.py:92
  718.3 0.6 copy-start.2
  1101.5 0.6 copy-start.4
  1482.5 0.6 copy-start.6
  1863.3 1.3 copy-start.8
  1868.1 8.1 copy-start.3
  1868.1 8.1 copy-start.5
  1868.2 8.1 copy-start.7
  1868.2 8.1 copy-start.9
  1876.2 2.0 copy-start.1
Sparse Core Ops, SparseCore 0:
  17.6 153.5 all-reduce.6
  192.0 145.6 all-reduce.8
where the time goes:
time: 1900 us; the launch traced here: 1890 us
  other arithmetic  685 us (36%)
  matrix products  455 us (24%)
  loops' own time  391 us (21%)
  waiting for transfers between devices  296 us (16%)
  local copies, waits for them, and re-layouts  43.5 us (2%)
    dot_general x523, matrix products, product(): jnp.dot(left, right, precision=lax.Precision.HIGHEST, preferred_element_t...  438 us
    another operation x4, loops' own time, small_upper(): return lax.fori_loop(0, width, one_step, start)[1]  377 us
    reduce_sum x512, other arithmetic, one_step(): pivot = jnp.sum(jnp.where(positions == index, row, jnp.float32(0.0)))  311 us
    reduce_sum x512, other arithmetic, one_step(): jnp.sum(jnp.where(positions == column, row, jnp.float32(0.0)))  310 us
    psum x1, waiting for transfers between devices, shards(): coeffs = lax.psum(inner(basis, block), ('leaf', 'side'))  150 us
    psum x1, waiting for transfers between devices, shards(): factor, inverse = factor_and_inverse(lax.psum(local_gram, ('leaf', 'side')))  146 us
    sub x512, other arithmetic, one_step(): rest = rest - new_row[:, None] * new_row[None, :]  42.1 us

commit v1 on v0

--- a/solution.py
+++ b/solution.py
@@ -85,11 +85,17 @@
 
 
 def shards(block, basis):
+
+    def _draft_group(page):
+        for hop_no in ("leaf", "side"):
+            page = lax.psum(page, hop_no)
+        return page
+
     rows_total = block.shape[0] * lax.axis_size("leaf") * lax.axis_size("side")
     coeffs = lax.psum(inner(basis, block), ("leaf", "side"))
     projected = block - product(basis, coeffs)
     local_gram = inner(projected, projected) / rows_total
-    factor, inverse = factor_and_inverse(lax.psum(local_gram, ("leaf", "side")))
+    factor, inverse = factor_and_inverse(_draft_group(local_gram))
     ortho = product(projected, inverse)
     return (ortho, factor, coeffs)
 

time: 1900 us -> 1840 us (0.968)
  matrix products: 455 us -> 426 us
  loops' own time: 391 us -> 362 us
    dot_general x523, matrix products: 438 us -> 409 us  [product(): jnp.dot(left, right, precision=lax.Precision.HIGHEST, preferred_element_t...]
    another operation x4, loops' own time: 377 us -> 348 us  [small_upper(): return lax.fori_loop(0, width, one_step, start)[1]]
    psum x1 -> x2, waiting for transfers between devices: 146 us -> 147 us  [_draft_group(): page = lax.psum(page, hop_no)]
where the time goes in v1:
time: 1840 us; the launch traced here: 1830 us
  other arithmetic  684 us (37%)
  matrix products  426 us (23%)
  loops' own time  362 us (20%)
  waiting for transfers between devices  298 us (16%)
  local copies, waits for them, and re-layouts  43.5 us (2%)
    dot_general x523, matrix products, product(): jnp.dot(left, right, precision=lax.Precision.HIGHEST, preferred_element_t...  409 us
    another operation x4, loops' own time, small_upper(): return lax.fori_loop(0, width, one_step, start)[1]  348 us
    reduce_sum x512, other arithmetic, one_step(): pivot = jnp.sum(jnp.where(positions == index, row, jnp.float32(0.0)))  310 us
    reduce_sum x512, other arithmetic, one_step(): jnp.sum(jnp.where(positions == column, row, jnp.float32(0.0)))  309 us
    psum x1, waiting for transfers between devices, shards(): coeffs = lax.psum(inner(basis, block), ('leaf', 'side'))  150 us
    psum x2, waiting for transfers between devices, _draft_group(): page = lax.psum(page, hop_no)  147 us
    sub x512, other arithmetic, one_step(): rest = rest - new_row[:, None] * new_row[None, :]  42.1 us

profile of v1, /device:TPU:1, one launch (start us, length us, event | category | flops | bytes accessed | tf_op | source)
XLA Modules:
  0.0 1827.6 jit_solution(16015379351258437922)
XLA Ops:
  7.2 10.2 fusion.74
  17.7 1.3 copy-done
  19.0 1.8 copy.5
  20.8 150.3 %all-reduce.8.cloned.1.call-done = f32[1024,512]{1,0:T(8,128)} async-done(((f32[1024,512]{1,0:T(8,128)}), f32[1024,512]{1,0:T(8,128)}) %all-reduce.8.cloned.1.call-update) | async-done | bytes 2097168 | tf_op jit(solution)/shard_map/psum | solution.py:95
  171.2 16.2 bitcast_subtract_fusion
  187.3 4.5 convolution_multiply_fusion
  192.1 83.5 %all-reduce.10.cloned.1.call-done = f32[512,512]{1,0:T(8,128)} async-done(((f32[512,512]{1,0:T(8,128)}), f32[512,512]{1,0:T(8,128)}) %all-reduce.10.cloned.1.call-update) | async-done | bytes 1048592 | tf_op jit(solution)/shard_map/psum | solution.py:91
  275.7 63.7 %all-reduce.12.cloned.1.call-done = f32[512,512]{1,0:T(8,128)} async-done(((f32[512,512]{1,0:T(8,128)}), f32[512,512]{1,0:T(8,128)}) %all-reduce.12.cloned.1.call-update) | async-done | bytes 1048592 | tf_op jit(solution)/shard_map/psum | solution.py:91
  339.4 0.8 slice.36
  340.3 175.1 %while.136 = (s32[]{:T(128)}, f32[128,128]{1,0:T(8,128)S(1)}, f32[128,128]{1,0:T(8,128)S(1)}, s32[]{:T(128)}, s32[]{:T(128)}) while((s32[]{:T(128)}, f32[128,128]{1,0:T(8,128)S(1)}, f32[128,128]{1,0:T(8,128)S(1)}, s32[]{:T(128)}, s32[]{:T(128)}) %tuple.273), condition=%wide.region_5.6_spmd.clone.clone, body=%wide.region_3.5_spmd.clone.clone.sunk | while | flops 34305 | bytes 142421 | solution.py:36
  515.4 169.7 %while.137 = (s32[]{:T(128)}, f32[128,128]{1,0:T(8,128)S(1)}, f32[128,128]{1,0:T(8,128)S(1)}, s32[]{:T(128)}, s32[]{:T(128)}, /*index=5*/s32[]{:T(128)}, s32[]{:T(128)}) while((s32[]{:T(128)}, f32[128,128]{1,0:T(8,128)S(1)}, f32[128,128]{1,0:T(8,128)S(1)}, s32[]{:T(128)}, s32[]{:T(128)}, /*index=5*/s32[]{:T(128)}, ...), condition=%wide.region_8.9_spmd.clone.clone, body=%wide.region_6.8_spmd.clone.clone.sunk | while | flops 197765 | bytes 69783 | solution.py:52
  685.7 1.3 fusion.63
  687.0 1.7 convolution_subtract_fusion
  688.8 176.4 %while.138 = (s32[]{:T(128)}, f32[128,128]{1,0:T(8,128)S(1)}, f32[128,128]{1,0:T(8,128)S(1)}, s32[]{:T(128)}, s32[]{:T(128)}) while((s32[]{:T(128)}, f32[128,128]{1,0:T(8,128)S(1)}, f32[128,128]{1,0:T(8,128)S(1)}, s32[]{:T(128)}, s32[]{:T(128)}) %tuple.279), condition=%wide.region_11.12_spmd.clone.clone, body=%wide.region_9.11_spmd.clone.clone.sunk | while | flops 34305 | bytes 142421 | solution.py:36
  865.2 171.0 %while.139 = (s32[]{:T(128)}, f32[128,128]{1,0:T(8,128)S(1)}, f32[128,128]{1,0:T(8,128)S(1)}, s32[]{:T(128)}, s32[]{:T(128)}, /*index=5*/s32[]{:T(128)}, s32[]{:T(128)}) while((s32[]{:T(128)}, f32[128,128]{1,0:T(8,128)S(1)}, f32[128,128]{1,0:T(8,128)S(1)}, s32[]{:T(128)}, s32[]{:T(128)}, /*index=5*/s32[]{:T(128)}, ...), condition=%wide.region_14.15_spmd.clone.clone, body=%wide.region_12.14_spmd.clone.clone.sunk | while | flops 197765 | bytes 69783 | solution.py:52
  1037.5 196.0 %while.140 = (s32[]{:T(128)}, f32[128,128]{1,0:T(8,128)S(1)}, f32[128,128]{1,0:T(8,128)S(1)}, s32[]{:T(128)}, s32[]{:T(128)}) while((s32[]{:T(128)}, f32[128,128]{1,0:T(8,128)S(1)}, f32[128,128]{1,0:T(8,128)S(1)}, s32[]{:T(128)}, s32[]{:T(128)}) %tuple.285), condition=%wide.region_17.18_spmd.clone.clone, body=%wide.region_15.17_spmd.clone.clone.sunk | while | flops 34305 | bytes 142421 | solution.py:36
  1233.5 190.6 %while.141 = (s32[]{:T(128)}, f32[128,128]{1,0:T(8,128)S(1)}, f32[128,128]{1,0:T(8,128)S(1)}, s32[]{:T(128)}, s32[]{:T(128)}, /*index=5*/s32[]{:T(128)}, s32[]{:T(128)}) while((s32[]{:T(128)}, f32[128,128]{1,0:T(8,128)S(1)}, f32[128,128]{1,0:T(8,128)S(1)}, s32[]{:T(128)}, s32[]{:T(128)}, /*index=5*/s32[]{:T(128)}, ...), condition=%wide.region_20.21_spmd.clone.clone, body=%wide.region_18.20_spmd.clone.clone.sunk | while | flops 197765 | bytes 69783 | solution.py:52
  1425.3 192.5 %while.142 = (s32[]{:T(128)}, f32[128,128]{1,0:T(8,128)S(1)}, f32[128,128]{1,0:T(8,128)S(1)}, s32[]{:T(128)}, s32[]{:T(128)}) while((s32[]{:T(128)}, f32[128,128]{1,0:T(8,128)S(1)}, f32[128,128]{1,0:T(8,128)S(1)}, s32[]{:T(128)}, s32[]{:T(128)}) %tuple.291), condition=%wide.region_23.24_spmd.clone.clone, body=%wide.region_21.23_spmd.clone.clone.sunk | while | flops 34305 | bytes 142421 | solution.py:36
  1617.9 187.1 %while.143 = (s32[]{:T(128)}, f32[128,128]{1,0:T(8,128)S(1)}, f32[128,128]{1,0:T(8,128)S(1)}, s32[]{:T(128)}, s32[]{:T(128)}, /*index=5*/s32[]{:T(128)}, s32[]{:T(128)}) while((s32[]{:T(128)}, f32[128,128]{1,0:T(8,128)S(1)}, f32[128,128]{1,0:T(8,128)S(1)}, s32[]{:T(128)}, s32[]{:T(128)}, /*index=5*/s32[]{:T(128)}, ...), condition=%wide.region_26.27_spmd.clone.clone, body=%wide.region_24.26_spmd.clone.clone.sunk | while | flops 197765 | bytes 69783 | solution.py:52
  1618.5 0.8 fusion.157
  1619.9 0.8 fusion.157
  1621.4 0.8 fusion.157
  1622.9 0.8 fusion.157
  1624.3 0.8 fusion.157
  1625.8 0.8 fusion.157
  1627.3 0.8 fusion.157
  1628.7 0.8 fusion.157
  1630.2 0.8 fusion.157
  1631.6 0.8 fusion.157
  1633.1 0.8 fusion.157
  1634.6 0.8 fusion.157
  1636.0 0.8 fusion.157
  1637.5 0.8 fusion.157
  1638.9 0.8 fusion.157
  1640.4 0.8 fusion.157
  1641.9 0.8 fusion.157
  1643.3 0.8 fusion.157
  1644.8 0.8 fusion.157
  1646.3 0.8 fusion.157
  1647.7 0.8 fusion.157
  1649.2 0.8 fusion.157
  1650.6 0.8 fusion.157
  1652.1 0.8 fusion.157
  1653.6 0.8 fusion.157
  1655.0 0.8 fusion.157
  1656.5 0.8 fusion.157
  1657.9 0.8 fusion.157
  1659.4 0.8 fusion.157
  1684.3 0.8 fusion.157
  1685.7 0.8 fusion.157
  1712.0 0.8 fusion.157
  1713.5 0.8 fusion.157
  1739.8 0.8 fusion.157
  1741.3 0.8 fusion.157
  1767.6 0.8 fusion.157
  1769.0 0.8 fusion.157
  1795.3 0.8 fusion.157
  1796.8 0.8 fusion.157
  1806.7 1.4 fusion.73
  1808.3 1.4 convolution_negate_fusion
  1809.8 8.0 fusion.56
  1817.8 1.1 select_maximum_fusion
  1818.9 0.8 copy-done.1
  1819.7 1.3 copy.84
  (4620 shorter events, 1070.9 us)
Async XLA Ops:
  7.2 164.0 %all-reduce.8.cloned.1.call-start = ((), (), s32[]{:S(2)}) async-start(), calls=%async_computation | async-start | bytes 4194304 | tf_op jit(solution)/shard_map/psum | solution.py:95
  17.4 1.6 copy-start
  17.4 258.2 %all-reduce.10.cloned.1.call-start = ((), (), s32[]{:S(2)}) async-start(), calls=%async_computation.1 | async-start | bytes 2097152 | tf_op jit(solution)/shard_map/psum | solution.py:91
  191.8 147.6 %all-reduce.12.cloned.1.call-start = ((), (), s32[]{:S(2)}) async-start(), calls=%async_computation.2 | async-start | bytes 2097152 | tf_op jit(solution)/shard_map/psum | solution.py:91
  685.1 0.6 copy-start.2
  1036.1 0.6 copy-start.4
  1424.1 0.6 copy-start.6
  1804.9 1.3 copy-start.8
  1809.7 8.1 copy-start.3
  1809.7 8.1 copy-start.5
  1809.8 8.1 copy-start.7
  1809.8 8.1 copy-start.9
  1817.8 2.0 copy-start.1
Sparse Core Ops, SparseCore 0:
  17.6 153.5 all-reduce.7
  192.0 83.6 all-reduce.9
  278.0 61.3 all-reduce.11
